TPU v7x, 512 devices: a whole 4x4x16 slice. The times are simulated.
512 devices in a mesh: mode: 64 (over y, z), rank: 8 (over x, core).
Axes of the slice: x: 4, y: 4, z: 16, core: 2. Of those that a mesh axis runs over, the one named last changes fastest.
Arguments:
- operator_cores: bfloat16 [2, 4, 4, 2048, 2048], P(None, None, None, 'mode'), may hold values from -0.26516504 to 0.26516504
- vector_cores: bfloat16 [2, 64, 64, 2048], P(None, 'rank', None, 'mode'), may hold values from -17 to 17
- left_gram: float32 [256, 256], replicated, may hold values from -330 to 330, as said below
- bases: float32 [3, 256, 64], replicated, may hold values from -0.375 to 0.375
Outputs:
- rounded_cores: float32 [2, 64, 2048, 64], P(None, None, ('mode', 'rank'))
- final_gram: float32 [256, 256], replicated
Inputs may be any that keep to these rules, and one draw needn't show every extreme that they name: left_gram is symmetric positive definite.
All inputs are finite; a program needn't handle non-finite values.
Results may differ from a plain program's by a relative error of at most 0.0028.
Values may be sent and summed in bfloat16 or wider, within the bound.
A program may use at most 64 MiB of HBM per device.

v0:
```python
import jax
import jax.numpy as jnp
from jax import lax
from jax.sharding import PartitionSpec as P

MODES = 2048
RANK = 256
HIGHEST_PRECISION = lax.Precision.HIGHEST


def solve_mixing(gram_now, basis):
    projected = jnp.dot(
        basis.T, gram_now, precision=HIGHEST_PRECISION, preferred_element_type=jnp.float32
    )
    reduced = jnp.dot(
        projected, basis, precision=HIGHEST_PRECISION, preferred_element_type=jnp.float32
    )
    reduced = 0.5 * (reduced + reduced.T)
    lower_factor = jnp.linalg.cholesky(reduced)
    return jax.scipy.linalg.cho_solve((lower_factor, True), projected)


def shards(operator_cores, vector_cores, left_gram, bases):
    gram_now = left_gram
    results = []
    core_count = operator_cores.shape[0]
    for core_index in range(core_count):
        mixing = solve_mixing(gram_now, bases[core_index])
        next_basis = bases[core_index + 1]
        operator_core = operator_cores[core_index]
        vector_core = vector_cores[core_index]
        local_rows = vector_core.shape[0]
        vector_width = vector_core.shape[1]
        operator_width = operator_core.shape[0]
        local_modes = operator_core.shape[2]
        gathered = lax.all_gather(vector_core, "mode", axis=2, tiled=True)
        product = jnp.einsum(
            "qsj,ptij->qpist", gathered, operator_core, preferred_element_type=jnp.float32
        )
        row_major = product.reshape(
            local_rows * operator_width, local_modes, vector_width * operator_width
        )
        row_major = row_major.astype(jnp.bfloat16)
        exchanged = lax.all_to_all(row_major, "rank", split_axis=1, concat_axis=0, tiled=True)
        widened = exchanged.astype(jnp.float32)
        weighted = jnp.einsum("ad,dib->aib", gram_now, widened, precision=HIGHEST_PRECISION)
        partial_gram = jnp.einsum("aib,aic->bc", widened, weighted, precision=HIGHEST_PRECISION) / (
            MODES * RANK
        )
        mixed = jnp.einsum("sa,aib->sib", mixing, widened, precision=HIGHEST_PRECISION)
        rounded_core = jnp.einsum("sib,bt->sit", mixed, next_basis, precision=HIGHEST_PRECISION)
        results.append(rounded_core)
        gram_now = lax.psum(partial_gram, ("mode", "rank"))
    return (jnp.stack(results), gram_now)


def solution(mesh):
    placed = (P(None, None, None, "mode", None), P(None, "rank", None, "mode"), P(), P())
    return jax.shard_map(
        shards,
        mesh=mesh,
        in_specs=placed,
        out_specs=(P(None, None, ("mode", "rank"), None), P()),
        check_vma=False,
    )
```

profile of v0, /device:TPU:4, one launch (start us, length us, event | category | flops | bytes accessed | tf_op | source)
XLA Modules:
  0.0 1263.4 jit_solution(10983501923882909832)
XLA Ops:
  7.2 0.9 fusion.62
  8.1 0.7 copy.55
  8.9 0.7 copy.56
  9.6 1.1 fusion.43
  10.7 1.0 fusion.41
  11.7 0.1 copy.28
  11.8 0.1 copy.29
  11.9 5.8 cholesky.44
  17.8 0.7 compare_reduce_fusion.1
  18.5 0.6 fusion.51
  19.1 4.9 custom-call.8
  24.0 0.3 fusion.58
  24.3 0.2 convolution_bitcast_fusion.6
  24.5 138.1 %all-gather.5.cloned.1.call-done = bf16[1,8,64,2048]{2,1,0,3:T(8,128)(2,1)} async-done(((bf16[1,8,64,32]{2,1,0,3:T(8,128)(2,1)}), bf16[1,8,64,2048]{2,1,0,3:T(8,128)(2,1)}) %all-gather.5.cloned.1.call-update) | async-done | bytes 2097168 | tf_op jit(solution)/shard_map/all_gather | solution.py:36
  162.6 4.5 copy.31
  167.1 3.9 fusion.23
  171.0 1.4 copy.32
  172.4 1.8 copy.33
  174.2 4.8 all-to-all-start
  179.0 128.4 %all-gather.7.cloned.1.call-done = bf16[1,8,64,2048]{2,1,0,3:T(8,128)(2,1)} async-done(((bf16[1,8,64,32]{2,1,0,3:T(8,128)(2,1)}), bf16[1,8,64,2048]{2,1,0,3:T(8,128)(2,1)}) %all-gather.7.cloned.1.call-update) | async-done | bytes 2097168 | tf_op jit(solution)/shard_map/all_gather | solution.py:36
  307.4 4.5 copy.41
  311.8 4.9 fusion.18
  316.8 2.9 copy.42
  319.7 1.8 copy.43
  321.4 4.8 all-to-all-start.1
  326.3 0.7 convolution_bitcast_fusion
  327.0 1.5 fusion.29
  328.5 0.2 all-reduce.5.cloned.1.call-start
  328.7 0.4 fusion.63
  329.1 4.3 all-to-all-done.1
  333.5 0.4 convolution_bitcast_fusion.4
  333.9 451.1 %all-reduce.3.cloned.1.call-done = f32[256,256]{1,0:T(8,128)} async-done(((f32[256,256]{1,0:T(8,128)}), f32[256,256]{1,0:T(8,128)}) %all-reduce.3.cloned.1.call-update) | async-done | bytes 262160 | tf_op jit(solution)/shard_map/psum | solution.py:53
  784.9 1.3 fusion.37
  786.2 0.2 fusion.39
  786.4 0.1 copy.38
  786.6 5.8 cholesky.55
  792.5 0.6 compare_reduce_fusion
  793.1 0.7 fusion.52
  793.8 4.9 custom-call.9
  798.7 0.3 fusion.34
  799.0 0.2 convolution_bitcast_fusion.5
  799.2 0.4 fusion.64
  799.6 0.6 fusion.30
  800.1 1.5 fusion.28
  801.7 0.4 convolution_bitcast_fusion.3
  802.1 0.9 copy.46
  802.9 452.2 %all-reduce.5.cloned.1.call-done = f32[256,256]{1,0:T(8,128)} async-done(((f32[256,256]{1,0:T(8,128)}), f32[256,256]{1,0:T(8,128)}) %all-reduce.5.cloned.1.call-update) | async-done | bytes 262160 | tf_op jit(solution)/shard_map/psum | solution.py:53
  1255.2 1.7 copy.59
  (24 shorter events, 0.5 us)
Async XLA Ops:
  7.2 2.4 copy-start
  7.2 155.4 %all-gather.5.cloned.1.call-start = ((), (), s32[]{:S(2)}) async-start(), calls=%async_computation.4 | async-start | bytes 4259840 | tf_op jit(solution)/shard_map/all_gather | solution.py:36
  8.8 298.6 %all-gather.7.cloned.1.call-start = ((), (), s32[]{:S(2)}) async-start(), calls=%async_computation.5 | async-start | bytes 4259840 | tf_op jit(solution)/shard_map/all_gather | solution.py:36
  174.2 147.2 %all-to-all-start = ((bf16[32,32,256]{2,0,1:T(8,128)(2,1)}), bf16[32,32,256]{2,0,1:T(8,128)(2,1)S(1)}, u32[]{:S(2)}, u32[]{:S(2)}) async-start(bf16[32,32,256]{2,0,1:T(8,128)(2,1)} %copy.33), calls=%async_computation | async-start | bytes 1048576 | tf_op jit(solution)/shard_map/all_to_all | solution.py:44
  321.4 12.0 all-to-all-start.1
  326.2 458.7 %all-reduce.3.cloned.1.call-start = ((), (), s32[]{:S(2)}) async-start(), calls=%async_computation.2 | async-start | bytes 524288 | tf_op jit(solution)/shard_map/psum | solution.py:53
  327.0 6.5 copy-start.2
  328.5 926.7 %all-reduce.5.cloned.1.call-start = ((), (), s32[]{:S(2)}) async-start(), calls=%async_computation.3 | async-start | bytes 524288 | tf_op jit(solution)/shard_map/psum | solution.py:53
  784.9 14.6 %copy-start.1 = (f32[256,256]{1,0:T(8,128)S(1)}, f32[256,256]{1,0:T(8,128)}, u32[]{:S(2)}) copy-start(f32[256,256]{1,0:T(8,128)} %all-reduce.3.cloned.1.call-done) | copy-start | bytes 786436
Sparse Core Ops, SparseCore 0:
  11.5 151.0 all-gather.4
  166.1 141.1 all-gather.6
  333.1 451.7 all-reduce.2
  801.8 453.3 all-reduce.4
where the time goes:
time: 1260 us
  waiting for transfers between devices  1170 us (93%)
  other arithmetic  24.2 us (2%)
  local copies, waits for them, and re-layouts  21.9 us (2%)
  matrix products  19.1 us (2%)
  between operations  14 us (1%)
    psum x2, waiting for transfers between devices, shards(): gram_now = lax.psum(partial_gram, ('mode', 'rank'))  903 us
    all_gather x2, waiting for transfers between devices, shards(): gathered = lax.all_gather(vector_core, 'mode', axis=2, tiled=True)  267 us
  transfers between devices with their start and end apart: 6, of which 5 were waited for; matrix products, arithmetic and copies ran while one was open for 4% of the time, Pallas kernels for 0%

commit v1 on v0

--- a/solution.py
+++ b/solution.py
@@ -33,7 +33,8 @@
         vector_width = vector_core.shape[1]
         operator_width = operator_core.shape[0]
         local_modes = operator_core.shape[2]
-        gathered = lax.all_gather(vector_core, "mode", axis=2, tiled=True)
+        copies = jnp.concatenate([vector_core] * lax.axis_size("mode"), axis=2)
+        gathered = lax.all_to_all(copies, "mode", 2, 2, tiled=True)
         product = jnp.einsum(
             "qsj,ptij->qpist", gathered, operator_core, preferred_element_type=jnp.float32
         )

time: 1260 us -> 1200 us (0.952)
  waiting for transfers between devices: 1170 us -> 1050 us
  local copies, waits for them, and re-layouts: 21.9 us -> 58.8 us
  starting transfers between devices: 9.91 us -> 37.3 us
    all_gather x2 -> x0, waiting for transfers between devices: 267 us -> none  [shards(): gathered = lax.all_gather(vector_core, 'mode', axis=2, tiled=True)]
    all_to_all x0 -> x2, waiting for transfers between devices: none -> 154 us  [shards(): gathered = lax.all_to_all(copies, 'mode', 2, 2, tiled=True)]
    unnamed x10 -> x148, local copies, waits for them, and re-layouts: 3.88 us -> 42.4 us
    all_to_all x0 -> x2, starting transfers between devices: none -> 27.3 us  [shards(): gathered = lax.all_to_all(copies, 'mode', 2, 2, tiled=True)]
  transfers between devices with their start and end apart: 6 -> 6, of which waited for: 5 -> 5; matrix products, arithmetic and copies ran while one was open for 4% -> 6% of each run, Pallas kernels for 0% -> 0%
where the time goes in v1:
time: 1200 us
  waiting for transfers between devices  1050 us (88%)
  local copies, waits for them, and re-layouts  58.8 us (5%)
  starting transfers between devices  37.3 us (3%)
  other arithmetic  24.2 us (2%)
  matrix products  15.1 us (1%)
  between operations  14.5 us (1%)
    psum x2, waiting for transfers between devices, shards(): gram_now = lax.psum(partial_gram, ('mode', 'rank'))  891 us
    all_to_all x2, waiting for transfers between devices, shards(): gathered = lax.all_to_all(copies, 'mode', 2, 2, tiled=True)  154 us
    unnamed x148, local copies, waits for them, and re-layouts  42.4 us
    all_to_all x2, starting transfers between devices, shards(): gathered = lax.all_to_all(copies, 'mode', 2, 2, tiled=True)  27.3 us
  transfers between devices with their start and end apart: 6, of which 5 were waited for; matrix products, arithmetic and copies ran while one was open for 6% of the time, Pallas kernels for 0%

profile of v1, /device:TPU:4, one launch (start us, length us, event | category | flops | bytes accessed | tf_op | source)
XLA Modules:
  0.0 1199.9 jit_solution(11114459517237921278)
XLA Ops:
  7.2 0.9 fusion.62
  13.3 1.9 copy-done.2
  15.3 2.0 copy-done.3
  17.3 7.9 reshape.30
  25.1 18.7 %all-to-all-start = ((bf16[64,2,8192]{2,1,0:T(2,128)(2,1)}), bf16[64,2,8192]{2,1,0:T(2,128)(2,1)S(1)}, u32[]{:S(2)}, u32[]{:S(2)}) async-start(bf16[64,2,8192]{2,1,0:T(2,128)(2,1)} %reshape.30), calls=%async_computation | async-start | bytes 4194304 | tf_op jit(solution)/shard_map/all_to_all | solution.py:37
  43.9 7.9 reshape.32
  51.8 89.3 %all-to-all-done = bf16[64,2,8192]{2,1,0:T(2,128)(2,1)S(1)} async-done(((bf16[64,2,8192]{2,1,0:T(2,128)(2,1)}), bf16[64,2,8192]{2,1,0:T(2,128)(2,1)S(1)}, u32[]{:S(2)}, u32[]{:S(2)}) %all-to-all-start) | async-done | bytes 2097184 | tf_op jit(solution)/shard_map/all_to_all | solution.py:37
  141.1 1.3 copy-done.1
  142.5 8.5 all-to-all-start.2
  151.7 5.8 cholesky.44
  157.6 0.6 compare_reduce_fusion.1
  158.2 0.7 fusion.51
  158.9 4.9 custom-call.8
  163.8 0.3 fusion.58
  164.2 7.9 reshape.31
  172.2 2.5 bitcast_bitcast_fusion.1
  174.7 0.9 copy-done.6
  175.6 2.3 fusion.23
  178.0 2.5 copy.32
  180.4 2.9 copy.33
  183.3 65.1 %all-to-all-done.2 = bf16[64,2,8192]{2,1,0:T(2,128)(2,1)S(1)} async-done(((bf16[64,2,8192]{2,1,0:T(2,128)(2,1)}), bf16[64,2,8192]{2,1,0:T(2,128)(2,1)S(1)}, u32[]{:S(2)}, u32[]{:S(2)}) %all-to-all-start.2) | async-done | bytes 2097184 | tf_op jit(solution)/shard_map/all_to_all | solution.py:37
  248.4 4.8 all-to-all-start.1
  253.2 4.0 reshape.33
  257.2 2.5 bitcast_bitcast_fusion
  259.8 0.9 copy-done.7
  260.7 3.3 fusion.18
  264.0 2.9 copy.42
  266.8 1.8 copy.43
  268.6 4.9 all-to-all-start.3
  273.6 0.7 convolution_bitcast_fusion
  274.3 1.5 fusion.29
  276.1 0.4 fusion.63
  276.5 4.3 all-to-all-done.3
  280.8 0.4 convolution_bitcast_fusion.4
  281.2 450.4 %all-reduce.3.cloned.1.call-done = f32[256,256]{1,0:T(8,128)} async-done(((f32[256,256]{1,0:T(8,128)}), f32[256,256]{1,0:T(8,128)}) %all-reduce.3.cloned.1.call-update) | async-done | bytes 262160 | tf_op jit(solution)/shard_map/psum | solution.py:54
  731.6 1.5 fusion.30
  733.1 1.5 fusion.28
  734.6 1.2 fusion.37
  736.2 5.8 cholesky.55
  742.1 0.6 compare_reduce_fusion
  742.8 0.7 fusion.52
  743.4 4.9 custom-call.9
  748.3 0.3 fusion.34
  748.8 0.4 fusion.64
  749.2 0.4 convolution_bitcast_fusion.3
  749.6 0.9 copy.46
  750.5 441.0 %all-reduce.5.cloned.1.call-done = f32[256,256]{1,0:T(8,128)} async-done(((f32[256,256]{1,0:T(8,128)}), f32[256,256]{1,0:T(8,128)}) %all-reduce.5.cloned.1.call-update) | async-done | bytes 262160 | tf_op jit(solution)/shard_map/psum | solution.py:54
  1191.4 1.7 copy.457
  (161 shorter events, 6.9 us)
Async XLA Ops:
  7.2 143.8 %copy-start = (f32[256,256]{1,0:T(8,128)S(1)}, f32[256,256]{1,0:T(8,128)}, u32[]{:S(2)}) copy-start(f32[256,256]{1,0:T(8,128)} %param.9) | copy-start | bytes 786436
  13.3 1.9 copy-start.2
  15.3 2.0 copy-start.3
  25.1 116.0 %all-to-all-start = ((bf16[64,2,8192]{2,1,0:T(2,128)(2,1)}), bf16[64,2,8192]{2,1,0:T(2,128)(2,1)S(1)}, u32[]{:S(2)}, u32[]{:S(2)}) async-start(bf16[64,2,8192]{2,1,0:T(2,128)(2,1)} %reshape.30), calls=%async_computation | async-start | bytes 4194304 | tf_op jit(solution)/shard_map/all_to_all | solution.py:37
  43.9 107.1 %copy-start.4 = (f32[3,256,64]{1,2,0:T(8,128)S(1)}, f32[3,256,64]{1,2,0:T(8,128)}, u32[]{:S(2)}) copy-start(f32[3,256,64]{1,2,0:T(8,128)} %param.10) | copy-start | bytes 589828
  141.1 1.3 copy-start.1
  142.5 105.9 %all-to-all-start.2 = ((bf16[64,2,8192]{2,1,0:T(2,128)(2,1)}), bf16[64,2,8192]{2,1,0:T(2,128)(2,1)S(1)}, u32[]{:S(2)}, u32[]{:S(2)}) async-start(bf16[64,2,8192]{2,1,0:T(2,128)(2,1)} %reshape.32), calls=%async_computation.2 | async-start | bytes 4194304 | tf_op jit(solution)/shard_map/all_to_all | solution.py:37
  172.2 3.4 copy-start.6
  248.4 20.2 %all-to-all-start.1 = ((bf16[32,32,256]{2,0,1:T(8,128)(2,1)}), bf16[32,32,256]{2,0,1:T(8,128)(2,1)S(1)}, u32[]{:S(2)}, u32[]{:S(2)}) async-start(bf16[32,32,256]{2,0,1:T(8,128)(2,1)} %copy.33), calls=%async_computation.1 | async-start | bytes 1048576 | tf_op jit(solution)/shard_map/all_to_all | solution.py:45
  257.2 3.4 copy-start.7
  268.6 12.2 %copy-start.5 = (f32[3,256,64]{1,2,0:T(8,128)S(1)}, f32[3,256,64]{1,2,0:T(8,128)}, u32[]{:S(2)}) copy-start(f32[3,256,64]{1,2,0:T(8,128)} %param.10) | copy-start | bytes 589828
  268.6 12.1 %all-to-all-start.3 = ((bf16[32,32,256]{2,0,1:T(8,128)(2,1)}), bf16[32,32,256]{2,0,1:T(8,128)(2,1)S(1)}, u32[]{:S(2)}, u32[]{:S(2)}) async-start(bf16[32,32,256]{2,0,1:T(8,128)(2,1)} %copy.43), calls=%async_computation.3 | async-start | bytes 1048576 | tf_op jit(solution)/shard_map/all_to_all | solution.py:45
  273.6 458.0 %all-reduce.3.cloned.1.call-start = ((), (), s32[]{:S(2)}) async-start(), calls=%async_computation.4 | async-start | bytes 524288 | tf_op jit(solution)/shard_map/psum | solution.py:54
  275.8 915.6 %all-reduce.5.cloned.1.call-start = ((), (), s32[]{:S(2)}) async-start(), calls=%async_computation.5 | async-start | bytes 524288 | tf_op jit(solution)/shard_map/psum | solution.py:54
Sparse Core Ops, SparseCore 0:
  280.4 451.1 all-reduce.2
  738.5 452.9 all-reduce.4

commit v2 on v0

--- a/solution.py
+++ b/solution.py
@@ -50,7 +50,7 @@
         mixed = jnp.einsum("sa,aib->sib", mixing, widened, precision=HIGHEST_PRECISION)
         rounded_core = jnp.einsum("sib,bt->sit", mixed, next_basis, precision=HIGHEST_PRECISION)
         results.append(rounded_core)
-        gram_now = lax.psum(partial_gram, ("mode", "rank"))
+        gram_now = lax.psum(lax.psum(partial_gram, "mode"), "rank")
     return (jnp.stack(results), gram_now)
 
 

time: 1260 us -> 1020 us (0.81)
  the two profiles are of different devices: /device:TPU:4 before, /device:TPU:8 now
where the time goes in v2:
time: 1020 us
  waiting for transfers between devices  930 us (91%)
  other arithmetic  24.1 us (2%)
  local copies, waits for them, and re-layouts  21.9 us (2%)
  matrix products  20 us (2%)
  between operations  14.4 us (1%)
    psum x4, waiting for transfers between devices, shards(): gram_now = lax.psum(lax.psum(partial_gram, 'mode'), 'rank')  664 us
    all_gather x2, waiting for transfers between devices, shards(): gathered = lax.all_gather(vector_core, 'mode', axis=2, tiled=True)  266 us
  transfers between devices with their start and end apart: 8, of which 6 were waited for; matrix products, arithmetic and copies ran while one was open for 4% of the time, Pallas kernels for 0%

profile of v2, /device:TPU:8, one launch (start us, length us, event | category | flops | bytes accessed | tf_op | source)
XLA Modules:
  0.0 1019.5 jit_solution(10153567072176903368)
XLA Ops:
  7.2 0.9 fusion.62
  8.1 0.7 copy.55
  8.9 0.7 copy.56
  9.6 1.1 fusion.43
  10.7 1.0 fusion.41
  11.7 0.1 copy.28
  11.9 5.8 cholesky.44
  17.8 0.6 compare_reduce_fusion.1
  18.5 0.6 fusion.51
  19.0 4.9 custom-call.8
  23.9 137.3 %all-gather.5.cloned.1.call-done = bf16[1,8,64,2048]{2,1,0,3:T(8,128)(2,1)} async-done(((bf16[1,8,64,32]{2,1,0,3:T(8,128)(2,1)}), bf16[1,8,64,2048]{2,1,0,3:T(8,128)(2,1)}) %all-gather.5.cloned.1.call-update) | async-done | bytes 2097168 | tf_op jit(solution)/shard_map/all_gather | solution.py:36
  161.2 4.5 copy.31
  165.7 3.9 fusion.23
  169.6 1.4 copy.32
  171.0 1.8 copy.33
  172.8 4.3 all-to-all-start
  177.1 128.9 %all-gather.7.cloned.1.call-done = bf16[1,8,64,2048]{2,1,0,3:T(8,128)(2,1)} async-done(((bf16[1,8,64,32]{2,1,0,3:T(8,128)(2,1)}), bf16[1,8,64,2048]{2,1,0,3:T(8,128)(2,1)}) %all-gather.7.cloned.1.call-update) | async-done | bytes 2097168 | tf_op jit(solution)/shard_map/all_gather | solution.py:36
  306.0 4.5 copy.41
  310.5 4.9 fusion.18
  315.4 2.9 copy.42
  318.3 1.8 copy.43
  320.0 4.3 all-to-all-start.1
  324.4 0.7 convolution_bitcast_fusion
  325.1 1.5 fusion.29
  326.7 0.3 fusion.58
  326.9 0.2 convolution_bitcast_fusion.6
  327.1 260.0 %all-reduce.5.cloned.1.call-done = f32[256,256]{1,0:T(8,128)} async-done(((f32[256,256]{1,0:T(8,128)}), f32[256,256]{1,0:T(8,128)}) %all-reduce.5.cloned.1.call-update) | async-done | bytes 262160 | tf_op jit(solution)/shard_map/psum | solution.py:53
  587.2 0.2 all-reduce.9.cloned.1.call-start
  587.4 0.4 fusion.63
  587.9 0.4 convolution_bitcast_fusion.4
  588.2 71.9 %all-reduce.7.cloned.1.call-done = f32[256,256]{1,0:T(8,128)} async-done(((f32[256,256]{1,0:T(8,128)}), f32[256,256]{1,0:T(8,128)}) %all-reduce.7.cloned.1.call-update) | async-done | bytes 262160 | tf_op jit(solution)/shard_map/psum | solution.py:53
  660.2 1.2 fusion.37
  661.4 0.2 fusion.39
  661.6 0.1 copy.38
  661.8 5.8 cholesky.55
  667.7 0.6 compare_reduce_fusion
  668.3 0.7 fusion.52
  669.0 4.9 custom-call.9
  673.9 0.3 fusion.34
  674.1 1.5 fusion.30
  675.7 1.5 fusion.28
  677.2 0.2 convolution_bitcast_fusion.5
  677.4 0.4 fusion.64
  677.8 260.2 %all-reduce.9.cloned.1.call-done = f32[256,256]{1,0:T(8,128)} async-done(((f32[256,256]{1,0:T(8,128)}), f32[256,256]{1,0:T(8,128)}) %all-reduce.9.cloned.1.call-update) | async-done | bytes 262160 | tf_op jit(solution)/shard_map/psum | solution.py:53
  938.0 0.4 convolution_bitcast_fusion.3
  938.4 0.9 copy.46
  939.3 71.7 %all-reduce.11.cloned.1.call-done = f32[256,256]{1,0:T(8,128)} async-done(((f32[256,256]{1,0:T(8,128)}), f32[256,256]{1,0:T(8,128)}) %all-reduce.11.cloned.1.call-update) | async-done | bytes 262160 | tf_op jit(solution)/shard_map/psum | solution.py:53
  1011.0 1.7 copy.61
  (28 shorter events, 0.7 us)
Async XLA Ops:
  7.2 2.4 copy-start
  7.2 154.1 %all-gather.5.cloned.1.call-start = ((), (), s32[]{:S(2)}) async-start(), calls=%async_computation.6 | async-start | bytes 4259840 | tf_op jit(solution)/shard_map/all_gather | solution.py:36
  8.8 297.2 %all-gather.7.cloned.1.call-start = ((), (), s32[]{:S(2)}) async-start(), calls=%async_computation.7 | async-start | bytes 4259840 | tf_op jit(solution)/shard_map/all_gather | solution.py:36
  172.8 147.2 %all-to-all-start = ((bf16[32,32,256]{2,0,1:T(8,128)(2,1)}), bf16[32,32,256]{2,0,1:T(8,128)(2,1)S(1)}, u32[]{:S(2)}, u32[]{:S(2)}) async-start(bf16[32,32,256]{2,0,1:T(8,128)(2,1)} %copy.33), calls=%async_computation | async-start | bytes 1048576 | tf_op jit(solution)/shard_map/all_to_all | solution.py:44
  320.0 267.7 %all-to-all-start.1 = ((bf16[32,32,256]{2,0,1:T(8,128)(2,1)}), bf16[32,32,256]{2,0,1:T(8,128)(2,1)S(1)}, u32[]{:S(2)}, u32[]{:S(2)}) async-start(bf16[32,32,256]{2,0,1:T(8,128)(2,1)} %copy.43), calls=%async_computation.1 | async-start | bytes 1048576 | tf_op jit(solution)/shard_map/all_to_all | solution.py:44
  324.3 262.8 %all-reduce.5.cloned.1.call-start = ((), (), s32[]{:S(2)}) async-start(), calls=%async_computation.2 | async-start | bytes 524288 | tf_op jit(solution)/shard_map/psum | solution.py:53
  325.1 262.7 %copy-start.1 = (f32[3,256,64]{1,2,0:T(8,128)S(1)}, f32[3,256,64]{1,2,0:T(8,128)}, u32[]{:S(2)}) copy-start(f32[3,256,64]{1,2,0:T(8,128)} %param.10) | copy-start | bytes 589828
  326.6 333.5 %all-reduce.7.cloned.1.call-start = ((), (), s32[]{:S(2)}) async-start(), calls=%async_computation.3 | async-start | bytes 524288 | tf_op jit(solution)/shard_map/psum | solution.py:53
  587.2 350.8 %all-reduce.9.cloned.1.call-start = ((), (), s32[]{:S(2)}) async-start(), calls=%async_computation.4 | async-start | bytes 524288 | tf_op jit(solution)/shard_map/psum | solution.py:53
  677.2 333.8 %all-reduce.11.cloned.1.call-start = ((), (), s32[]{:S(2)}) async-start(), calls=%async_computation.5 | async-start | bytes 524288 | tf_op jit(solution)/shard_map/psum | solution.py:53
Sparse Core Ops, SparseCore 0:
  11.5 149.6 all-gather.4
  164.8 141.1 all-gather.6
  329.1 257.9 all-reduce.4
  589.4 70.6 all-reduce.6
  677.3 260.6 all-reduce.8
  940.3 70.6 all-reduce.10
